TPU v7x, 32 devices: a whole 2x2x4 slice. The times are simulated.
32 devices in a mesh: dp: 8 (over y, x, core), tensor: 4 (over z).
Axes of the slice: x: 2, y: 2, z: 4, core: 2. Of those that a mesh axis runs over, the one named last changes fastest.
Arguments:
- inputs: bfloat16 [8192, 1536], P(('dp', 'tensor')), may hold values from -12 to 12
- norm1_gain: float32 [1536], replicated, may hold values from 0.5 to 1.5
- w_in_x: bfloat16 [1536, 2048], P('dp', 'tensor'), may hold values from -0.15625 to 0.15625
- w_in_y: bfloat16 [1536, 2048], P('dp', 'tensor'), may hold values from -0.15625 to 0.15625
- conv_w: float32 [4, 2048], P(None, 'tensor'), may hold values from -3 to 3
- conv_b: float32 [2048], P('tensor'), may hold values from -1.8 to 1.8
- gates: bfloat16 [2, 16, 128, 128], P(None, 'tensor', 'dp'), may hold values from -0.5 to 0.5
- gate_bias: float32 [2, 2048], P(None, 'tensor'), may hold values from -1 to 1
- decay_param: float32 [2048], P('tensor'), may hold values from -7 to -1
- w_out: bfloat16 [1536, 2048], P('dp', 'tensor'), may hold values from -0.375 to 0.375
- norm2_gain: float32 [1536], replicated, may hold values from 0.5 to 1.5
- w_gate: bfloat16 [1536, 4608], P('dp', 'tensor'), may hold values from -0.15625 to 0.15625
- w_up: bfloat16 [1536, 4608], P('dp', 'tensor'), may hold values from -0.15625 to 0.15625
- w_down: bfloat16 [1536, 4608], P('dp', 'tensor'), may hold values from -0.125 to 0.125
- cotangent: bfloat16 [8192, 1536], P(('dp', 'tensor')), may hold values from -6 to 6
Outputs:
- output: bfloat16 [8192, 1536], P(('dp', 'tensor'))
- grad_inputs: bfloat16 [8192, 1536], P(('dp', 'tensor'))
- grad_norm1_gain: float32 [1536], replicated
- grad_w_in_x: float32 [1536, 2048], P('dp', 'tensor')
- grad_w_in_y: float32 [1536, 2048], P('dp', 'tensor')
- grad_conv_w: float32 [4, 2048], replicated
- grad_conv_b: float32 [2048], replicated
- grad_gates: float32 [2, 16, 128, 128], P(None, 'tensor', 'dp')
- grad_gate_bias: float32 [2, 2048], replicated
- grad_decay_param: float32 [2048], replicated
- grad_w_out: float32 [1536, 2048], P('dp', 'tensor')
- grad_norm2_gain: float32 [1536], replicated
- grad_w_gate: float32 [1536, 4608], P('dp', 'tensor')
- grad_w_up: float32 [1536, 4608], P('dp', 'tensor')
- grad_w_down: float32 [1536, 4608], P('dp', 'tensor')
- stream_rms: float32 [4], replicated
All inputs are finite; a program needn't handle non-finite values.
Results may differ from a plain program's by a relative error of at most 0.0085.
Values may be sent and summed in bfloat16 or wider, within the bound.
A program may use at most 192 MiB of HBM per device.

v0:
```python
import jax
import jax.numpy as jnp
from jax import lax
from jax.sharding import PartitionSpec as P

CONV = 4
SEQ_LEN = 1024
epsilon = 1e-06


def gelu_tanh(value):
    return jax.nn.gelu(value, approximate=True)


def combine(earlier, later):
    return (earlier[0] * later[0], later[0] * earlier[1] + later[1])


def norm_back(value, scale, gain, grad):
    scaled = gain * grad
    return scale * scaled - value * scale * scale * scale * jnp.mean(
        scaled * value, axis=1, keepdims=True
    )


def row_product(left, right):
    return lax.dot_general(
        left, right, (((0,), (0,)), ((), ())), preferred_element_type=jnp.float32
    )


def back_product(left, right):
    return lax.dot_general(
        left, right, (((1,), (1,)), ((), ())), preferred_element_type=jnp.float32
    )


def local(
    inputs,
    norm1_gain,
    w_in_x,
    w_in_y,
    conv_w,
    conv_b,
    gates,
    gate_bias,
    decay_param,
    w_out,
    norm2_gain,
    w_gate,
    w_up,
    w_down,
    cotangent,
):
    row_count = inputs.shape[0]
    model_width = inputs.shape[1]
    tensor_count = lax.axis_size("tensor")
    group_rows = row_count * tensor_count
    seq_count = group_rows // SEQ_LEN
    rec_x, rec_y, rec_o, gate_mats = (
        lax.all_gather(w_in_x, "dp", axis=0, tiled=True),
        lax.all_gather(w_in_y, "dp", axis=0, tiled=True),
        lax.all_gather(w_out, "dp", axis=0, tiled=True),
        lax.all_gather(gates, "dp", axis=2, tiled=True),
    )
    channels = rec_x.shape[1]
    blocks_here = gate_mats.shape[1]
    block_width = gate_mats.shape[3]
    residual = inputs.astype(jnp.float32)
    scale_one = lax.rsqrt(jnp.mean(residual * residual, axis=1, keepdims=True) + epsilon)
    n_one = (residual * scale_one * norm1_gain).astype(jnp.bfloat16)
    full_one = lax.all_gather(n_one, "tensor", axis=0, tiled=True)
    x_branch = jnp.dot(full_one, rec_x, preferred_element_type=jnp.float32)
    y_pre = jnp.dot(full_one, rec_y, preferred_element_type=jnp.float32)
    seq_x = x_branch.reshape(seq_count, SEQ_LEN, channels)
    padded = jnp.pad(seq_x, ((0, 0), (CONV - 1, 0), (0, 0)))
    conv_sum = conv_b + jnp.zeros_like(seq_x)
    for k in range(CONV):
        conv_sum = conv_sum + conv_w[k] * padded[:, CONV - 1 - k : CONV - 1 - k + SEQ_LEN]
    conv_low = conv_sum.reshape(group_rows, channels).astype(jnp.bfloat16)
    conv_value = conv_low.astype(jnp.float32)
    blocked = conv_low.reshape(group_rows, blocks_here, block_width)
    z_input = (
        jnp.einsum(
            "gbi,bij->gbj", blocked, gate_mats[0], preferred_element_type=jnp.float32
        ).reshape(group_rows, channels)
        + gate_bias[0]
    )
    z_decay = (
        jnp.einsum(
            "gbi,bij->gbj", blocked, gate_mats[1], preferred_element_type=jnp.float32
        ).reshape(group_rows, channels)
        + gate_bias[1]
    )
    seq_start = (jnp.arange(group_rows) % SEQ_LEN == 0)[:, None]

    def coefficients(input_pre, decay_pre, conv_part, decay_raw):
        log_decay = -8.0 * jax.nn.sigmoid(decay_pre) * jax.nn.softplus(decay_raw)
        mult = jnp.where(seq_start, 1.0, jnp.sqrt(-jnp.expm1(2.0 * log_decay)))
        return (jnp.exp(log_decay), mult * jax.nn.sigmoid(input_pre) * conv_part)

    (decays, inflow), pull_coeff = jax.vjp(coefficients, z_input, z_decay, conv_value, decay_param)
    seq_decay = decays.reshape(seq_count, SEQ_LEN, channels)
    _, seq_states = lax.associative_scan(
        combine, (seq_decay, inflow.reshape(seq_count, SEQ_LEN, channels)), axis=1
    )
    states = seq_states.reshape(group_rows, channels)
    y_gate = gelu_tanh(y_pre)
    mixed_out = (states * y_gate).astype(jnp.bfloat16)
    branch = lax.psum_scatter(
        back_product(mixed_out, rec_o), "tensor", scatter_dimension=0, tiled=True
    )
    stream = residual + branch
    mlp_g, mlp_u, mlp_d = (
        lax.all_gather(w_gate, "dp", axis=0, tiled=True),
        lax.all_gather(w_up, "dp", axis=0, tiled=True),
        lax.all_gather(w_down, "dp", axis=0, tiled=True),
    )
    scale_two = lax.rsqrt(jnp.mean(stream * stream, axis=1, keepdims=True) + epsilon)
    n_two = (stream * scale_two * norm2_gain).astype(jnp.bfloat16)
    full_two = lax.all_gather(n_two, "tensor", axis=0, tiled=True)
    gate_pre = jnp.dot(full_two, mlp_g, preferred_element_type=jnp.float32)
    up_pre = jnp.dot(full_two, mlp_u, preferred_element_type=jnp.float32)
    hidden = (gelu_tanh(gate_pre) * up_pre).astype(jnp.bfloat16)
    ffn_out = lax.psum_scatter(
        back_product(hidden, mlp_d), "tensor", scatter_dimension=0, tiled=True
    )
    result = stream + ffn_out
    output = result.astype(jnp.bfloat16)
    squares = jnp.stack(
        [
            jnp.sum(stream * stream),
            jnp.sum(branch * branch),
            jnp.sum(ffn_out * ffn_out),
            jnp.sum(result * result),
        ]
    )
    upstream = cotangent.astype(jnp.float32)
    full_cot = lax.all_gather(cotangent, "tensor", axis=0, tiled=True)
    d_hidden = jnp.dot(full_cot, mlp_d, preferred_element_type=jnp.float32)
    grad_down = row_product(full_cot, hidden)
    _, pull_mlp = jax.vjp(
        lambda gate_value, up_value: gelu_tanh(gate_value) * up_value, gate_pre, up_pre
    )
    d_gate, d_up = pull_mlp(d_hidden)
    d_gate_low = d_gate.astype(jnp.bfloat16)
    d_up_low = d_up.astype(jnp.bfloat16)
    grad_gate_w = row_product(full_two, d_gate_low)
    grad_up_w = row_product(full_two, d_up_low)
    d_two = lax.psum_scatter(
        back_product(d_gate_low, mlp_g) + back_product(d_up_low, mlp_u),
        "tensor",
        scatter_dimension=0,
        tiled=True,
    )
    grad_gain_two = jnp.sum(d_two * stream * scale_two, axis=0)
    d_stream = upstream + norm_back(stream, scale_two, norm2_gain, d_two)
    mlp_summed = (grad_gate_w, grad_up_w, grad_down)
    full_branch = lax.all_gather(d_stream.astype(jnp.bfloat16), "tensor", axis=0, tiled=True)
    d_mixed = jnp.dot(full_branch, rec_o, preferred_element_type=jnp.float32)
    grad_out_w = row_product(full_branch, mixed_out)
    d_states = d_mixed * y_gate
    _, pull_gelu = jax.vjp(gelu_tanh, y_pre)
    d_y_low = pull_gelu(d_mixed * states)[0].astype(jnp.bfloat16)
    next_decay = jnp.concatenate([seq_decay[:, 1:], jnp.zeros_like(seq_decay[:, :1])], axis=1)
    _, carried = lax.associative_scan(
        combine, (next_decay, d_states.reshape(seq_count, SEQ_LEN, channels)), reverse=True, axis=1
    )
    prev_states = jnp.concatenate([jnp.zeros_like(seq_states[:, :1]), seq_states[:, :-1]], axis=1)
    d_decays = (carried * prev_states).reshape(group_rows, channels)
    d_input_pre, d_decay_pre, d_conv_direct, grad_decay = pull_coeff(
        (d_decays, carried.reshape(group_rows, channels))
    )
    d_input_low = d_input_pre.astype(jnp.bfloat16)
    d_decay_low = d_decay_pre.astype(jnp.bfloat16)
    grad_bias = jnp.stack(
        [
            jnp.sum(d_input_low, axis=0, dtype=jnp.float32),
            jnp.sum(d_decay_low, axis=0, dtype=jnp.float32),
        ]
    )
    input_blocks = d_input_low.reshape(group_rows, blocks_here, block_width)
    decay_blocks = d_decay_low.reshape(group_rows, blocks_here, block_width)
    grad_gate_mats = jnp.stack(
        [
            jnp.einsum("gbi,gbj->bij", blocked, input_blocks, preferred_element_type=jnp.float32),
            jnp.einsum("gbi,gbj->bij", blocked, decay_blocks, preferred_element_type=jnp.float32),
        ]
    )
    d_conv = d_conv_direct + jnp.einsum(
        "gbj,bij->gbi", input_blocks, gate_mats[0], preferred_element_type=jnp.float32
    ).reshape(group_rows, channels)
    d_conv = d_conv + jnp.einsum(
        "gbj,bij->gbi", decay_blocks, gate_mats[1], preferred_element_type=jnp.float32
    ).reshape(group_rows, channels)
    seq_dconv = d_conv.reshape(seq_count, SEQ_LEN, channels)
    grad_conv_b = jnp.sum(seq_dconv, axis=(0, 1))
    padded_back = jnp.pad(seq_dconv, ((0, 0), (0, CONV - 1), (0, 0)))
    tap_grads = []
    d_x_seq = jnp.zeros_like(seq_dconv)
    for k in range(CONV):
        tap_grads.append(
            jnp.sum(seq_dconv * padded[:, CONV - 1 - k : CONV - 1 - k + SEQ_LEN], axis=(0, 1))
        )
        d_x_seq = d_x_seq + conv_w[k] * padded_back[:, k : k + SEQ_LEN]
    grad_conv_w = jnp.stack(tap_grads)
    d_x_low = d_x_seq.reshape(group_rows, channels).astype(jnp.bfloat16)
    grad_in_x_w = row_product(full_one, d_x_low)
    grad_in_y_w = row_product(full_one, d_y_low)
    d_one = lax.psum_scatter(
        back_product(d_x_low, rec_x) + back_product(d_y_low, rec_y),
        "tensor",
        scatter_dimension=0,
        tiled=True,
    )
    grad_gain_one = jnp.sum(d_one * residual * scale_one, axis=0)
    grad_inputs = (d_stream + norm_back(residual, scale_one, norm1_gain, d_one)).astype(
        jnp.bfloat16
    )
    small_grads = jnp.concatenate(
        [grad_conv_w, grad_conv_b[None], grad_bias, grad_decay[None]], axis=0
    )
    spread_grads = lax.dynamic_update_slice(
        jnp.zeros((small_grads.shape[0], channels * tensor_count), jnp.float32),
        small_grads,
        (0, lax.axis_index("tensor") * channels),
    )
    gain_total, small_total, square_total = lax.psum(
        (jnp.stack([grad_gain_one, grad_gain_two]), spread_grads, squares), ("dp", "tensor")
    )
    stream_rms = jnp.sqrt(
        square_total / (row_count * lax.axis_size("dp") * tensor_count * model_width)
    )
    summed_all = (
        lax.psum_scatter(grad_in_x_w, "dp", scatter_dimension=0, tiled=True),
        lax.psum_scatter(grad_in_y_w, "dp", scatter_dimension=0, tiled=True),
        lax.psum_scatter(grad_out_w, "dp", scatter_dimension=0, tiled=True),
        lax.psum_scatter(grad_gate_mats, "dp", scatter_dimension=2, tiled=True),
        lax.psum_scatter(mlp_summed[0], "dp", scatter_dimension=0, tiled=True),
        lax.psum_scatter(mlp_summed[1], "dp", scatter_dimension=0, tiled=True),
        lax.psum_scatter(mlp_summed[2], "dp", scatter_dimension=0, tiled=True),
    )
    rec_summed = summed_all[:4]
    grad_gate_sum, grad_up_sum, grad_down_sum = (summed_all[4], summed_all[5], summed_all[6])
    return (
        output,
        grad_inputs,
        gain_total[0],
        rec_summed[0],
        rec_summed[1],
        small_total[0:CONV],
        small_total[CONV],
        rec_summed[3],
        small_total[CONV + 1 : CONV + 3],
        small_total[CONV + 3],
        rec_summed[2],
        gain_total[1],
        grad_gate_sum,
        grad_up_sum,
        grad_down_sum,
        stream_rms,
    )


def solution(mesh):
    return jax.shard_map(
        local,
        mesh=mesh,
        in_specs=(
            P(("dp", "tensor"), None),
            P(),
            P("dp", "tensor"),
            P("dp", "tensor"),
            P(None, "tensor"),
            P("tensor"),
            P(None, "tensor", "dp", None),
            P(None, "tensor"),
            P("tensor"),
            P("dp", "tensor"),
            P(),
            P("dp", "tensor"),
            P("dp", "tensor"),
            P("dp", "tensor"),
            P(("dp", "tensor"), None),
        ),
        out_specs=(
            P(("dp", "tensor"), None),
            P(("dp", "tensor"), None),
            P(),
            P("dp", "tensor"),
            P("dp", "tensor"),
            P(),
            P(),
            P(None, "tensor", "dp", None),
            P(),
            P(),
            P("dp", "tensor"),
            P(),
            P("dp", "tensor"),
            P("dp", "tensor"),
            P("dp", "tensor"),
            P(),
        ),
        check_vma=False,
    )
```

profile of v0, /device:TPU:0, one launch (start us, length us, event | category | flops | bytes accessed | tf_op | source)
XLA Modules:
  0.0 1922.4 jit_solution(16737749595569484958)
XLA Ops:
  13.7 11.2 all_gather.35
  26.0 12.7 all-gather.13.cloned.1.call-done
  38.7 65.7 %all-gather.11.cloned.1.call-done = bf16[1024,1536]{1,0:T(8,128)(2,1)} async-done(((bf16[256,1536]{1,0:T(8,128)(2,1)}), bf16[1024,1536]{1,0:T(8,128)(2,1)}) %all-gather.11.cloned.1.call-update) | async-done | bytes 3145744 | tf_op jit(solution)/shard_map/all_gather | solution.py:72
  124.8 6.3 slice.563
  257.9 6.4 slice.561
  264.3 6.3 slice.634
  307.0 8.6 pad.152
  319.4 8.7 pad.151
  328.1 7.5 fusion.34
  342.5 108.9 %reduce-scatter.14.cloned.1.call-done = f32[256,1536]{1,0:T(8,128)} async-done(((f32[1024,1536]{1,0:T(8,128)}), f32[256,1536]{1,0:T(8,128)}) %reduce-scatter.14.cloned.1.call-update) | async-done | bytes 1572880 | tf_op jit(solution)/shard_map/reduce_scatter | solution.py:110
  458.6 29.1 %all-gather.21.cloned.1.call-done = bf16[1536,1152]{1,0:T(8,128)(2,1)} async-done(((bf16[192,1152]{1,0:T(8,128)(2,1)}), bf16[1536,1152]{1,0:T(8,128)(2,1)}) %all-gather.21.cloned.1.call-update) | async-done | bytes 3538960 | tf_op jit(solution)/shard_map/all_gather | solution.py:115
  487.7 65.7 %all-gather.19.cloned.1.call-done = bf16[1024,1536]{1,0:T(8,128)(2,1)} async-done(((bf16[256,1536]{1,0:T(8,128)(2,1)}), bf16[1024,1536]{1,0:T(8,128)(2,1)}) %all-gather.19.cloned.1.call-update) | async-done | bytes 3145744 | tf_op jit(solution)/shard_map/all_gather | solution.py:121
  553.4 9.3 fusion.131
  562.7 25.2 %all-gather.23.cloned.1.call-done = bf16[1536,1152]{1,0:T(8,128)(2,1)} async-done(((bf16[192,1152]{1,0:T(8,128)(2,1)}), bf16[1536,1152]{1,0:T(8,128)(2,1)}) %all-gather.23.cloned.1.call-update) | async-done | bytes 3538960 | tf_op jit(solution)/shard_map/all_gather | solution.py:116
  587.9 9.4 fusion.132
  597.3 55.7 %all-gather.27.cloned.1.call-done = bf16[1024,1536]{1,0:T(8,128)(2,1)} async-done(((bf16[256,1536]{1,0:T(8,128)(2,1)}), bf16[1024,1536]{1,0:T(8,128)(2,1)}) %all-gather.27.cloned.1.call-update) | async-done | bytes 3145744 | tf_op jit(solution)/shard_map/all_gather | solution.py:139
  653.0 34.4 %all-gather.25.cloned.1.call-done = bf16[1536,1152]{1,0:T(8,128)(2,1)} async-done(((bf16[192,1152]{1,0:T(8,128)(2,1)}), bf16[1536,1152]{1,0:T(8,128)(2,1)}) %all-gather.25.cloned.1.call-update) | async-done | bytes 3538960 | tf_op jit(solution)/shard_map/all_gather | solution.py:117
  687.4 13.0 multiply_convert_fusion
  704.8 6.3 convolution_add_fusion.1
  711.1 9.6 fusion.133
  720.8 101.2 %reduce-scatter.18.cloned.1.call-done = f32[256,1536]{1,0:T(8,128)} async-done(((f32[1024,1536]{1,0:T(8,128)}), f32[256,1536]{1,0:T(8,128)}) %reduce-scatter.18.cloned.1.call-update) | async-done | bytes 1572880 | tf_op jit(solution)/shard_map/reduce_scatter | solution.py:150
  822.0 113.4 %reduce-scatter.16.cloned.1.call-done = f32[256,1536]{1,0:T(8,128)} async-done(((f32[1024,1536]{1,0:T(8,128)}), f32[256,1536]{1,0:T(8,128)}) %reduce-scatter.16.cloned.1.call-update) | async-done | bytes 1572880 | tf_op jit(solution)/shard_map/reduce_scatter | solution.py:125
  945.5 6.5 slice.639
  964.5 8.9 slice.640
  973.4 8.9 slice.645
  982.3 9.2 slice.638
  1006.3 8.9 fusion.25
  1015.3 16.6 reverse.6
  1153.8 6.3 slice.713
  1196.7 8.6 pad.172
  1209.1 8.7 pad.171
  1221.8 16.7 rev.8
  1248.4 7.0 convert_reduce_fusion.1
  1270.5 8.6 multiply_reduce_fusion.1
  1299.3 9.9 fusion.137
  1309.3 9.9 fusion.138
  1319.4 9.4 convolution_bitcast_fusion
  1328.8 8.1 copy.95
  1362.0 40.5 %all-reduce.47.cloned.1.call-done = f32[8,2048]{1,0:T(8,128)} async-done(((f32[8,2048]{1,0:T(8,128)}), f32[8,2048]{1,0:T(8,128)}) %all-reduce.47.cloned.1.call-update) | async-done | bytes 65552 | tf_op jit(solution)/shard_map/psum | solution.py:228
  1407.0 109.3 %reduce-scatter.20.cloned.1.call-done = f32[256,1536]{1,0:T(8,128)} async-done(((f32[1024,1536]{1,0:T(8,128)}), f32[256,1536]{1,0:T(8,128)}) %reduce-scatter.20.cloned.1.call-update) | async-done | bytes 1572880 | tf_op jit(solution)/shard_map/reduce_scatter | solution.py:210
  1518.1 41.2 %all-reduce.44 = (f32[2,1536]{1,0:T(2,128)S(1)}, f32[4]{0:T(128)S(1)}) all-reduce(f32[2,1536]{1,0:T(2,128)S(1)} %pad_maximum_fusion.15, f32[4]{0:T(128)S(1)} %pad_maximum_fusion.20), channel_id=1, replica_groups=mesh['dp'=8,'tensor'=4] {'dp','tensor'}, use_global_device_ids=true, to_apply=%region_10.11 | all-reduce | flops 3076 | bytes 24608 | tf_op jit(solution)/shard_map/psum | solution.py:228
  1564.3 22.5 %reduce-scatter.30.cloned.1.call-done = f32[192,1152]{1,0:T(8,128)} async-done(((f32[1536,1152]{1,0:T(8,128)}), f32[192,1152]{1,0:T(8,128)}) %reduce-scatter.30.cloned.1.call-update) | async-done | bytes 884752 | tf_op jit(solution)/shard_map/reduce_scatter | solution.py:239
  1586.9 69.9 %reduce-scatter.32.cloned.1.call-done = f32[192,1152]{1,0:T(8,128)} async-done(((f32[1536,1152]{1,0:T(8,128)}), f32[192,1152]{1,0:T(8,128)}) %reduce-scatter.32.cloned.1.call-update) | async-done | bytes 884752 | tf_op jit(solution)/shard_map/reduce_scatter | solution.py:240
  1656.8 69.5 %reduce-scatter.34.cloned.1.call-done = f32[192,1152]{1,0:T(8,128)} async-done(((f32[1536,1152]{1,0:T(8,128)}), f32[192,1152]{1,0:T(8,128)}) %reduce-scatter.34.cloned.1.call-update) | async-done | bytes 884752
  1726.2 38.1 %reduce-scatter.26.cloned.1.call-done = f32[2,4,16,128]{3,2,1,0:T(8,128)} async-done(((f32[2,4,128,128]{3,2,1,0:T(8,128)}), f32[2,4,16,128]{3,2,1,0:T(8,128)}) %reduce-scatter.26.cloned.1.call-update) | async-done | bytes 65552 | tf_op jit(solution)/shard_map/reduce_scatter | solution.py:238
  1764.3 50.1 %reduce-scatter.22.cloned.1.call-done = f32[192,512]{1,0:T(8,128)} async-done(((f32[1536,512]{1,0:T(8,128)}), f32[192,512]{1,0:T(8,128)}) %reduce-scatter.22.cloned.1.call-update) | async-done | bytes 393232 | tf_op jit(solution)/shard_map/reduce_scatter | solution.py:235
  1814.4 50.6 %reduce-scatter.28.cloned.1.call-done = f32[192,512]{1,0:T(8,128)} async-done(((f32[1536,512]{1,0:T(8,128)}), f32[192,512]{1,0:T(8,128)}) %reduce-scatter.28.cloned.1.call-update) | async-done | bytes 393232 | tf_op jit(solution)/shard_map/reduce_scatter | solution.py:237
  1865.0 50.2 %reduce-scatter.24.cloned.1.call-done = f32[192,512]{1,0:T(8,128)} async-done(((f32[1536,512]{1,0:T(8,128)}), f32[192,512]{1,0:T(8,128)}) %reduce-scatter.24.cloned.1.call-update) | async-done | bytes 393232 | tf_op jit(solution)/shard_map/reduce_scatter | solution.py:236
  (523 shorter events, 497.7 us)
Async XLA Ops:
  7.2 31.5 %all-gather.13.cloned.1.call-start = ((), (), s32[]{:S(2)}) async-start(), calls=%async_computation.12 | async-start | bytes 1769472 | tf_op jit(solution)/shard_map/all_gather | solution.py:61
  7.9 96.4 %all-gather.11.cloned.1.call-start = ((), (), s32[]{:S(2)}) async-start(), calls=%async_computation.11 | async-start | bytes 3932160 | tf_op jit(solution)/shard_map/all_gather | solution.py:72
  11.7 316.4 %all-gather.15.cloned.1.call-start = ((), (), s32[]{:S(2)}) async-start(), calls=%async_computation.13 | async-start | bytes 1769472 | tf_op jit(solution)/shard_map/all_gather | solution.py:62
  12.4 323.2 %all-gather.17.cloned.1.call-start = ((), (), s32[]{:S(2)}) async-start(), calls=%async_computation.14 | async-start | bytes 1769472 | tf_op jit(solution)/shard_map/all_gather | solution.py:63
  13.0 438.4 %reduce-scatter.14.cloned.1.call-start = ((), (), s32[]{:S(2)}) async-start(), calls=%async_computation.15 | async-start | bytes 7864320 | tf_op jit(solution)/shard_map/reduce_scatter | solution.py:110
  13.6 94.9 %copy-start.50 = (f32[1,512]{1,0:T(1,128)}, f32[1,512]{1,0:T(1,128)S(1)}, u32[]{:S(2)}) copy-start(f32[1,512]{1,0:T(1,128)S(1)} %get-tuple-element.125) | copy-start | bytes 6148
  13.6 94.9 %copy-start.52 = (f32[1,512]{1,0:T(1,128)}, f32[1,512]{1,0:T(1,128)S(1)}, u32[]{:S(2)}) copy-start(f32[1,512]{1,0:T(1,128)S(1)} %get-tuple-element.126) | copy-start | bytes 6148
  13.6 94.9 %copy-start.54 = (f32[1,512]{1,0:T(1,128)}, f32[1,512]{1,0:T(1,128)S(1)}, u32[]{:S(2)}) copy-start(f32[1,512]{1,0:T(1,128)S(1)} %get-tuple-element.127) | copy-start | bytes 6148
  13.6 94.9 %copy-start.56 = (f32[1,512]{1,0:T(1,128)}, f32[1,512]{1,0:T(1,128)S(1)}, u32[]{:S(2)}) copy-start(f32[1,512]{1,0:T(1,128)S(1)} %get-tuple-element.128) | copy-start | bytes 6148
  25.3 89.0 %copy-start.23 = (bf16[1,4,128,128]{2,3,1,0:T(8,128)(2,1)}, bf16[1,4,128,128]{2,3,1,0:T(8,128)(2,1)S(1)}, u32[]{:S(2)}) copy-start(bf16[1,4,128,128]{2,3,1,0:T(8,128)(2,1)S(1)} %copy.98) | copy-start | bytes 393220
  25.3 93.6 %copy-start.34 = (f32[1,512]{1,0:T(1,128)}, f32[1,512]{1,0:T(1,128)S(1)}, u32[]{:S(2)}) copy-start(f32[1,512]{1,0:T(1,128)S(1)} %get-tuple-element.133) | copy-start | bytes 6148
  25.4 93.6 %copy-start.39 = (f32[1,512]{1,0:T(1,128)}, f32[1,512]{1,0:T(1,128)S(1)}, u32[]{:S(2)}) copy-start(f32[1,512]{1,0:T(1,128)S(1)} %get-tuple-element.134) | copy-start | bytes 6148
  26.0 93.0 %copy-start.41 = (f32[512]{0:T(512)}, f32[512]{0:T(512)S(1)}, u32[]{:S(2)}) copy-start(f32[512]{0:T(512)S(1)} %get-tuple-element.139) | copy-start | bytes 6148
  26.0 83.9 %copy-start.87 = (f32[512]{0:T(512)S(1)}, f32[512]{0:T(512)}, u32[]{:S(2)}) copy-start(f32[512]{0:T(512)} %param.20) | copy-start | bytes 6148
  341.9 113.5 %copy-start.28 = (f32[1536]{0:T(1024)S(1)}, f32[1536]{0:T(1024)}, u32[]{:S(2)}) copy-start(f32[1536]{0:T(1024)} %param.25) | copy-start | bytes 18436
  341.9 145.8 %all-gather.21.cloned.1.call-start = ((), (), s32[]{:S(2)}) async-start(), calls=%async_computation.17 | async-start | bytes 3981312 | tf_op jit(solution)/shard_map/all_gather | solution.py:115
  342.5 210.9 %all-gather.19.cloned.1.call-start = ((), (), s32[]{:S(2)}) async-start(), calls=%async_computation.16 | async-start | bytes 3932160 | tf_op jit(solution)/shard_map/all_gather | solution.py:121
  454.2 486.4 %copy-start.48 = (f32[256]{0:T(256)}, f32[256]{0:T(256)S(1)}, u32[]{:S(2)}) copy-start(f32[256]{0:T(256)S(1)} %add_rsqrt_fusion) | copy-start | bytes 3076
  456.5 131.5 %all-gather.23.cloned.1.call-start = ((), (), s32[]{:S(2)}) async-start(), calls=%async_computation.18 | async-start | bytes 3981312 | tf_op jit(solution)/shard_map/all_gather | solution.py:116
  457.2 195.8 %all-gather.27.cloned.1.call-start = ((), (), s32[]{:S(2)}) async-start(), calls=%async_computation.21 | async-start | bytes 3932160 | tf_op jit(solution)/shard_map/all_gather | solution.py:139
  457.9 229.5 %all-gather.25.cloned.1.call-start = ((), (), s32[]{:S(2)}) async-start(), calls=%async_computation.19 | async-start | bytes 3981312 | tf_op jit(solution)/shard_map/all_gather | solution.py:117
  458.5 363.5 %reduce-scatter.18.cloned.1.call-start = ((), (), s32[]{:S(2)}) async-start(), calls=%async_computation.22 | async-start | bytes 7864320 | tf_op jit(solution)/shard_map/reduce_scatter | solution.py:150
  711.1 224.4 %reduce-scatter.16.cloned.1.call-start = ((), (), s32[]{:S(2)}) async-start(), calls=%async_computation.20 | async-start | bytes 7864320 | tf_op jit(solution)/shard_map/reduce_scatter | solution.py:125
  720.7 285.6 %all-gather.29.cloned.1.call-start = ((), (), s32[]{:S(2)}) async-start(), calls=%async_computation.23 | async-start | bytes 3932160 | tf_op jit(solution)/shard_map/all_gather | solution.py:159
  942.1 460.4 %all-reduce.47.cloned.1.call-start = ((), (), s32[]{:S(2)}) async-start(), calls=%async_computation.27 | async-start | bytes 131072 | tf_op jit(solution)/shard_map/psum | solution.py:228
  1145.0 16.4 copy-start.61
  1145.0 16.4 copy-start.84
  1145.0 16.4 copy-start.85
  1145.0 16.5 copy-start.46
  1145.0 16.5 copy-start.80
  1145.1 16.6 copy-start.37
  1145.1 16.6 copy-start.38
  1145.1 16.6 copy-start.78
  1286.2 230.1 %reduce-scatter.20.cloned.1.call-start = ((), (), s32[]{:S(2)}) async-start(), calls=%async_computation.24 | async-start | bytes 7864320 | tf_op jit(solution)/shard_map/reduce_scatter | solution.py:210
  1299.3 287.6 %reduce-scatter.30.cloned.1.call-start = ((), (), s32[]{:S(2)}) async-start(), calls=%async_computation.30 | async-start | bytes 7962624 | tf_op jit(solution)/shard_map/reduce_scatter | solution.py:239
  1309.2 347.5 %reduce-scatter.32.cloned.1.call-start = ((), (), s32[]{:S(2)}) async-start(), calls=%async_computation.31 | async-start | bytes 7962624 | tf_op jit(solution)/shard_map/reduce_scatter | solution.py:240
  1319.2 407.1 %reduce-scatter.34.cloned.1.call-start = ((), (), s32[]{:S(2)}) async-start(), calls=%async_computation.32 | async-start | bytes 7962624
  1336.9 427.4 %reduce-scatter.26.cloned.1.call-start = ((), (), s32[]{:S(2)}) async-start(), calls=%async_computation.28 | async-start | bytes 589824 | tf_op jit(solution)/shard_map/reduce_scatter | solution.py:238
  1339.9 474.5 %reduce-scatter.22.cloned.1.call-start = ((), (), s32[]{:S(2)}) async-start(), calls=%async_computation.25 | async-start | bytes 3538944 | tf_op jit(solution)/shard_map/reduce_scatter | solution.py:235
  1345.3 519.7 %reduce-scatter.28.cloned.1.call-start = ((), (), s32[]{:S(2)}) async-start(), calls=%async_computation.29 | async-start | bytes 3538944 | tf_op jit(solution)/shard_map/reduce_scatter | solution.py:237
  1351.9 563.3 %reduce-scatter.24.cloned.1.call-start = ((), (), s32[]{:S(2)}) async-start(), calls=%async_computation.26 | async-start | bytes 3538944 | tf_op jit(solution)/shard_map/reduce_scatter | solution.py:236
  1358.5 157.8 %copy-start.6 = (bf16[256,1536]{1,0:T(8,128)(2,1)S(1)}, bf16[256,1536]{1,0:T(8,128)(2,1)}, u32[]{:S(2)}) copy-start(bf16[256,1536]{1,0:T(8,128)(2,1)} %param.15) | copy-start | bytes 2359300
  1358.5 157.8 %copy-start.33 = (f32[1536]{0:T(1024)S(1)}, f32[1536]{0:T(1024)}, u32[]{:S(2)}) copy-start(f32[1536]{0:T(1024)} %param.16) | copy-start | bytes 18436
  1358.5 157.8 %copy-start.63 = (f32[256]{0:T(256)S(1)}, f32[256]{0:T(256)}, u32[]{:S(2)}) copy-start(f32[256]{0:T(256)} %copy-done.62) | copy-start | bytes 3076
  1358.5 202.0 %copy-start.3 = (f32[256,1536]{1,0:T(8,128)S(1)}, f32[256,1536]{1,0:T(8,128)}, u32[]{:S(2)}) copy-start(f32[256,1536]{1,0:T(8,128)} %copy-done.1) | copy-start | bytes 4718596
  1358.5 202.0 %copy-start.19 = (bf16[256,1536]{1,0:T(8,128)(2,1)S(1)}, bf16[256,1536]{1,0:T(8,128)(2,1)}, u32[]{:S(2)}) copy-start(bf16[256,1536]{1,0:T(8,128)(2,1)} %param.29) | copy-start | bytes 2359300
  1358.5 202.0 %copy-start.49 = (f32[256]{0:T(256)S(1)}, f32[256]{0:T(256)}, u32[]{:S(2)}) copy-start(f32[256]{0:T(256)} %copy-done.48) | copy-start | bytes 3076
  1358.5 202.0 %copy-start.65 = (f32[256]{0:T(256)S(1)}, f32[256]{0:T(256)}, u32[]{:S(2)}) copy-start(f32[256]{0:T(256)} %copy-done.64) | copy-start | bytes 3076
  (67 other events, 460.1 us)
Sparse Core Ops, SparseCore 0:
  9.9 28.7 all-gather.12
  40.8 63.4 all-gather.10
  106.3 24.3 all-gather.14
  132.4 25.6 all-gather.16
  342.0 109.3 reduce-scatter.13
  453.2 34.4 all-gather.20
  489.9 63.4 all-gather.18
  555.3 32.6 all-gather.22
  589.5 63.4 all-gather.26
  654.8 32.6 all-gather.24
  711.2 110.7 reduce-scatter.17
  824.2 111.2 reduce-scatter.15
  942.3 64.0 all-gather.28
  1286.3 116.1 all-reduce.46
  1404.7 111.5 reduce-scatter.19
  1520.2 66.5 reduce-scatter.29
  1591.2 65.4 reduce-scatter.31
  1660.7 65.4 reduce-scatter.33
  1730.2 34.1 reduce-scatter.25
  1768.1 46.2 reduce-scatter.21
  1818.7 46.2 reduce-scatter.27
  1868.9 46.2 reduce-scatter.23
where the time goes:
time: 1950 us; the launch traced here: 1920 us
  waiting for transfers between devices  1120 us (57%)
  local copies, waits for them, and re-layouts  442 us (23%)
  other arithmetic  150 us (8%)
  matrix products  138 us (7%)
  blocking collectives  52.4 us (3%)
    slice x63, local copies, waits for them, and re-layouts, local(): lax.associative_scan(combine, (next_decay, d_states.reshape(seq_count, SE...  156 us
    slice x60, local copies, waits for them, and re-layouts, local(): lax.associative_scan(combine, (seq_decay, inflow.reshape(seq_count, SEQ_L...  127 us
    reduce_scatter x1, waiting for transfers between devices, local(): lax.psum_scatter(back_product(hidden, mlp_d), 'tensor', scatter_dimension...  113 us
    reduce_scatter x1, waiting for transfers between devices, local(): lax.psum_scatter(back_product(d_x_low, rec_x) + back_product(d_y_low, rec...  109 us
    reduce_scatter x1, waiting for transfers between devices, local(): lax.psum_scatter(back_product(mixed_out, rec_o), 'tensor', scatter_dimens...  109 us
    reduce_scatter x1, waiting for transfers between devices, local(): lax.psum_scatter(back_product(d_gate_low, mlp_g) + back_product(d_up_low,...  101 us
    unnamed x23, waiting for transfers between devices  74 us
    reduce_scatter x1, waiting for transfers between devices, local(): lax.psum_scatter(mlp_summed[1], 'dp', scatter_dimension=0, tiled=True)  69.9 us
  transfers between devices with their start and end apart: 22, of which 20 were waited for; matrix products, arithmetic and copies ran while one was open for 21% of the time, Pallas kernels for 0%

commit v1 on v0

--- a/solution.py
+++ b/solution.py
@@ -6,6 +6,27 @@
 CONV = 4
 SEQ_LEN = 1024
 epsilon = 1e-06
+
+
+def collect(x, axis, dim):
+    peers, index, rows = (lax.axis_size(axis), lax.axis_index(axis), x.shape[dim])
+    right = [(i, (i + 1) % peers) for i in range(peers)]
+    backward = [(i, (i - 1) % peers) for i in range(peers)]
+    filled = jnp.zeros((*x.shape[:dim], peers * rows, *x.shape[dim + 1 :]), x.dtype)
+    filled = lax.dynamic_update_slice_in_dim(filled, x, index * rows, axis=dim)
+    from_left = from_right = x
+    half = peers // 2
+    for step in range(1, half + 1):
+        from_left = lax.ppermute(from_left, axis, right)
+        filled = lax.dynamic_update_slice_in_dim(
+            filled, from_left, (index - step) % peers * rows, axis=dim
+        )
+        if step < peers - half:
+            from_right = lax.ppermute(from_right, axis, backward)
+            filled = lax.dynamic_update_slice_in_dim(
+                filled, from_right, (index + step) % peers * rows, axis=dim
+            )
+    return filled
 
 
 def gelu_tanh(value):
@@ -136,7 +157,7 @@
         ]
     )
     upstream = cotangent.astype(jnp.float32)
-    full_cot = lax.all_gather(cotangent, "tensor", axis=0, tiled=True)
+    full_cot = collect(cotangent, "tensor", 0)
     d_hidden = jnp.dot(full_cot, mlp_d, preferred_element_type=jnp.float32)
     grad_down = row_product(full_cot, hidden)
     _, pull_mlp = jax.vjp(

time: 1950 us -> 1880 us (0.964)
  waiting for transfers between devices: 1120 us -> 1050 us
    unnamed x23 -> x21, waiting for transfers between devices: 74 us -> 4.03 us
    reduce_scatter x0 -> x1, waiting for transfers between devices: none -> 69.5 us  [local(): lax.psum_scatter(mlp_summed[2], 'dp', scatter_dimension=0, tiled=True)]
    all_gather x1 -> x0, waiting for transfers between devices: 55.7 us -> none  [local(): full_cot = lax.all_gather(cotangent, 'tensor', axis=0, tiled=True)]
    ppermute x0 -> x3, waiting for transfers between devices: none -> 42 us  [the longest x2 42 us: collect(): from_left = lax.ppermute(from_left, axis, right)]
    all_gather x1, waiting for transfers between devices: 29.1 us -> 0.01 us  [local(): lax.all_gather(w_gate, 'dp', axis=0, tiled=True)]
    all_gather x1, waiting for transfers between devices: 65.7 us -> 37 us  [local(): full_two = lax.all_gather(n_two, 'tensor', axis=0, tiled=True)]
  transfers between devices with their start and end apart: 22 -> 24, of which waited for: 20 -> 20; matrix products, arithmetic and copies ran while one was open for 21% -> 22% of each run, Pallas kernels for 0% -> 0%
where the time goes in v1:
time: 1880 us; the launch traced here: 1860 us
  waiting for transfers between devices  1050 us (56%)
  local copies, waits for them, and re-layouts  432 us (23%)
  other arithmetic  148 us (8%)
  matrix products  138 us (7%)
  blocking collectives  52.6 us (3%)
  starting transfers between devices  19.7 us (1%)
    slice x63, local copies, waits for them, and re-layouts, local(): lax.associative_scan(combine, (next_decay, d_states.reshape(seq_count, SE...  152 us
    slice x60, local copies, waits for them, and re-layouts, local(): lax.associative_scan(combine, (seq_decay, inflow.reshape(seq_count, SEQ_L...  123 us
    reduce_scatter x1, waiting for transfers between devices, local(): lax.psum_scatter(back_product(hidden, mlp_d), 'tensor', scatter_dimension...  114 us
    reduce_scatter x1, waiting for transfers between devices, local(): lax.psum_scatter(back_product(d_x_low, rec_x) + back_product(d_y_low, rec...  109 us
    reduce_scatter x1, waiting for transfers between devices, local(): lax.psum_scatter(back_product(mixed_out, rec_o), 'tensor', scatter_dimens...  109 us
    reduce_scatter x1, waiting for transfers between devices, local(): lax.psum_scatter(back_product(d_gate_low, mlp_g) + back_product(d_up_low,...  101 us
    reduce_scatter x1, waiting for transfers between devices, local(): lax.psum_scatter(mlp_summed[1], 'dp', scatter_dimension=0, tiled=True)  69.9 us
    reduce_scatter x1, waiting for transfers between devices, local(): lax.psum_scatter(mlp_summed[2], 'dp', scatter_dimension=0, tiled=True)  69.5 us
  transfers between devices with their start and end apart: 24, of which 20 were waited for; matrix products, arithmetic and copies ran while one was open for 22% of the time, Pallas kernels for 0%

profile of v1, /device:TPU:0, one launch (start us, length us, event | category | flops | bytes accessed | tf_op | source)
XLA Modules:
  0.0 1858.9 jit_solution(4707918545061709262)
XLA Ops:
  13.2 11.4 all_gather.32
  25.6 13.1 all-gather.12.cloned.1.call-done
  38.7 65.7 %all-gather.10.cloned.1.call-done = bf16[1024,1536]{1,0:T(8,128)(2,1)} async-done(((bf16[256,1536]{1,0:T(8,128)(2,1)}), bf16[1024,1536]{1,0:T(8,128)(2,1)}) %all-gather.10.cloned.1.call-update) | async-done | bytes 3145744 | tf_op jit(solution)/shard_map/all_gather | solution.py:93
  143.5 6.3 slice.566
  253.7 6.4 slice.561
  260.1 6.3 slice.634
  301.2 8.6 pad.152
  313.6 8.7 pad.151
  322.3 7.5 fusion.34
  336.6 108.9 %reduce-scatter.12.cloned.1.call-done = f32[256,1536]{1,0:T(8,128)} async-done(((f32[1024,1536]{1,0:T(8,128)}), f32[256,1536]{1,0:T(8,128)}) %reduce-scatter.12.cloned.1.call-update) | async-done | bytes 1572880 | tf_op jit(solution)/shard_map/reduce_scatter | solution.py:131
  455.9 18.8 %collective-permute-done = bf16[256,1536]{1,0:T(8,128)(2,1)} collective-permute-done((bf16[256,1536]{1,0:T(8,128)(2,1)}, bf16[256,1536]{1,0:T(8,128)(2,1)}, u32[]{:S(2)}, u32[]{:S(2)}) %collective-permute-start) | collective-permute-done | bytes 786464 | tf_op jit(solution)/shard_map/ppermute | solution.py:20
  474.7 14.6 collective-permute-start.2
  496.2 23.3 %collective-permute-done.2 = bf16[256,1536]{1,0:T(8,128)(2,1)} collective-permute-done((bf16[256,1536]{1,0:T(8,128)(2,1)}, bf16[256,1536]{1,0:T(8,128)(2,1)}, u32[]{:S(2)}, u32[]{:S(2)}) %collective-permute-start.2) | collective-permute-done | bytes 786464 | tf_op jit(solution)/shard_map/ppermute | solution.py:20
  521.5 37.0 %all-gather.18.cloned.1.call-done = bf16[1024,1536]{1,0:T(8,128)(2,1)} async-done(((bf16[256,1536]{1,0:T(8,128)(2,1)}), bf16[1024,1536]{1,0:T(8,128)(2,1)}) %all-gather.18.cloned.1.call-update) | async-done | bytes 3145744 | tf_op jit(solution)/shard_map/all_gather | solution.py:142
  558.6 9.4 fusion.131
  567.9 25.8 %all-gather.22.cloned.1.call-done = bf16[1536,1152]{1,0:T(8,128)(2,1)} async-done(((bf16[192,1152]{1,0:T(8,128)(2,1)}), bf16[1536,1152]{1,0:T(8,128)(2,1)}) %all-gather.22.cloned.1.call-update) | async-done | bytes 3538960 | tf_op jit(solution)/shard_map/all_gather | solution.py:137
  593.7 9.4 fusion.132
  603.2 26.5 %all-gather.24.cloned.1.call-done = bf16[1536,1152]{1,0:T(8,128)(2,1)} async-done(((bf16[192,1152]{1,0:T(8,128)(2,1)}), bf16[1536,1152]{1,0:T(8,128)(2,1)}) %all-gather.24.cloned.1.call-update) | async-done | bytes 3538960 | tf_op jit(solution)/shard_map/all_gather | solution.py:138
  629.6 13.0 multiply_convert_fusion
  653.2 9.7 fusion.133
  663.0 101.1 %reduce-scatter.16.cloned.1.call-done = f32[256,1536]{1,0:T(8,128)} async-done(((f32[1024,1536]{1,0:T(8,128)}), f32[256,1536]{1,0:T(8,128)}) %reduce-scatter.16.cloned.1.call-update) | async-done | bytes 1572880 | tf_op jit(solution)/shard_map/reduce_scatter | solution.py:171
  764.1 113.6 %reduce-scatter.14.cloned.1.call-done = f32[256,1536]{1,0:T(8,128)} async-done(((f32[1024,1536]{1,0:T(8,128)}), f32[256,1536]{1,0:T(8,128)}) %reduce-scatter.14.cloned.1.call-update) | async-done | bytes 1572880 | tf_op jit(solution)/shard_map/reduce_scatter | solution.py:146
  887.8 6.5 slice.639
  894.2 6.3 slice.644
  906.8 8.9 slice.640
  915.7 8.9 slice.645
  924.6 9.1 slice.638
  948.6 9.1 fusion.25
  957.6 16.6 reverse.6
  1092.4 6.3 slice.713
  1133.4 8.8 pad.172
  1145.9 8.6 pad.171
  1158.5 16.6 rev.8
  1185.1 7.0 convert_reduce_fusion.1
  1207.2 8.8 multiply_reduce_fusion.1
  1236.1 9.8 fusion.137
  1246.0 9.8 fusion.138
  1256.1 9.8 fusion.139
  1291.1 48.1 %all-reduce.47.cloned.1.call-done = f32[8,2048]{1,0:T(8,128)} async-done(((f32[8,2048]{1,0:T(8,128)}), f32[8,2048]{1,0:T(8,128)}) %all-reduce.47.cloned.1.call-update) | async-done | bytes 65552 | tf_op jit(solution)/shard_map/psum | solution.py:249
  1343.7 109.3 %reduce-scatter.18.cloned.1.call-done = f32[256,1536]{1,0:T(8,128)} async-done(((f32[1024,1536]{1,0:T(8,128)}), f32[256,1536]{1,0:T(8,128)}) %reduce-scatter.18.cloned.1.call-update) | async-done | bytes 1572880 | tf_op jit(solution)/shard_map/reduce_scatter | solution.py:231
  1454.8 41.2 %all-reduce.44 = (f32[2,1536]{1,0:T(2,128)S(1)}, f32[4]{0:T(128)S(1)}) all-reduce(f32[2,1536]{1,0:T(2,128)S(1)} %pad_maximum_fusion.15, f32[4]{0:T(128)S(1)} %pad_maximum_fusion.20), channel_id=1, replica_groups=mesh['dp'=8,'tensor'=4] {'dp','tensor'}, use_global_device_ids=true, to_apply=%region_10.11 | all-reduce | flops 3076 | bytes 24608 | tf_op jit(solution)/shard_map/psum | solution.py:249
  1501.0 22.5 %reduce-scatter.28.cloned.1.call-done = f32[192,1152]{1,0:T(8,128)} async-done(((f32[1536,1152]{1,0:T(8,128)}), f32[192,1152]{1,0:T(8,128)}) %reduce-scatter.28.cloned.1.call-update) | async-done | bytes 884752 | tf_op jit(solution)/shard_map/reduce_scatter | solution.py:260
  1523.5 69.9 %reduce-scatter.30.cloned.1.call-done = f32[192,1152]{1,0:T(8,128)} async-done(((f32[1536,1152]{1,0:T(8,128)}), f32[192,1152]{1,0:T(8,128)}) %reduce-scatter.30.cloned.1.call-update) | async-done | bytes 884752 | tf_op jit(solution)/shard_map/reduce_scatter | solution.py:261
  1593.4 69.5 %reduce-scatter.32.cloned.1.call-done = f32[192,1152]{1,0:T(8,128)} async-done(((f32[1536,1152]{1,0:T(8,128)}), f32[192,1152]{1,0:T(8,128)}) %reduce-scatter.32.cloned.1.call-update) | async-done | bytes 884752 | tf_op jit(solution)/shard_map/reduce_scatter | solution.py:262
  1662.9 37.9 %reduce-scatter.24.cloned.1.call-done = f32[2,4,16,128]{3,2,1,0:T(8,128)} async-done(((f32[2,4,128,128]{3,2,1,0:T(8,128)}), f32[2,4,16,128]{3,2,1,0:T(8,128)}) %reduce-scatter.24.cloned.1.call-update) | async-done | bytes 65552 | tf_op jit(solution)/shard_map/reduce_scatter | solution.py:259
  1700.8 50.2 %reduce-scatter.20.cloned.1.call-done = f32[192,512]{1,0:T(8,128)} async-done(((f32[1536,512]{1,0:T(8,128)}), f32[192,512]{1,0:T(8,128)}) %reduce-scatter.20.cloned.1.call-update) | async-done | bytes 393232 | tf_op jit(solution)/shard_map/reduce_scatter | solution.py:256
  1751.0 50.5 %reduce-scatter.26.cloned.1.call-done = f32[192,512]{1,0:T(8,128)} async-done(((f32[1536,512]{1,0:T(8,128)}), f32[192,512]{1,0:T(8,128)}) %reduce-scatter.26.cloned.1.call-update) | async-done | bytes 393232 | tf_op jit(solution)/shard_map/reduce_scatter | solution.py:258
  1801.5 50.2 %reduce-scatter.22.cloned.1.call-done = f32[192,512]{1,0:T(8,128)} async-done(((f32[1536,512]{1,0:T(8,128)}), f32[192,512]{1,0:T(8,128)}) %reduce-scatter.22.cloned.1.call-update) | async-done | bytes 393232 | tf_op jit(solution)/shard_map/reduce_scatter | solution.py:257
  (536 shorter events, 497.7 us)
Async XLA Ops:
  7.2 31.5 %all-gather.12.cloned.1.call-start = ((), (), s32[]{:S(2)}) async-start(), calls=%async_computation.12 | async-start | bytes 1769472 | tf_op jit(solution)/shard_map/all_gather | solution.py:82
  7.9 96.4 %all-gather.10.cloned.1.call-start = ((), (), s32[]{:S(2)}) async-start(), calls=%async_computation.11 | async-start | bytes 3932160 | tf_op jit(solution)/shard_map/all_gather | solution.py:93
  11.7 310.6 %all-gather.14.cloned.1.call-start = ((), (), s32[]{:S(2)}) async-start(), calls=%async_computation.13 | async-start | bytes 1769472 | tf_op jit(solution)/shard_map/all_gather | solution.py:83
  12.4 317.3 %all-gather.16.cloned.1.call-start = ((), (), s32[]{:S(2)}) async-start(), calls=%async_computation.14 | async-start | bytes 1769472 | tf_op jit(solution)/shard_map/all_gather | solution.py:84
  13.0 432.5 %reduce-scatter.12.cloned.1.call-start = ((), (), s32[]{:S(2)}) async-start(), calls=%async_computation.15 | async-start | bytes 7864320 | tf_op jit(solution)/shard_map/reduce_scatter | solution.py:131
  13.1 105.8 %copy-start.61 = (pred[1024]{0:T(1024)(128)(4,1)}, pred[1024]{0:T(1024)(128)(4,1)S(1)}, u32[]{:S(2)}) copy-start(pred[1024]{0:T(1024)(128)(4,1)S(1)} %fusion.88) | copy-start | bytes 3076
  13.1 95.4 %copy-start.53 = (f32[1,512]{1,0:T(1,128)}, f32[1,512]{1,0:T(1,128)S(1)}, u32[]{:S(2)}) copy-start(f32[1,512]{1,0:T(1,128)S(1)} %get-tuple-element.93) | copy-start | bytes 6148
  13.1 95.4 %copy-start.55 = (f32[1,512]{1,0:T(1,128)}, f32[1,512]{1,0:T(1,128)S(1)}, u32[]{:S(2)}) copy-start(f32[1,512]{1,0:T(1,128)S(1)} %get-tuple-element.94) | copy-start | bytes 6148
  13.1 95.4 %copy-start.57 = (f32[1,512]{1,0:T(1,128)}, f32[1,512]{1,0:T(1,128)S(1)}, u32[]{:S(2)}) copy-start(f32[1,512]{1,0:T(1,128)S(1)} %get-tuple-element.95) | copy-start | bytes 6148
  13.1 95.4 %copy-start.59 = (f32[1,512]{1,0:T(1,128)}, f32[1,512]{1,0:T(1,128)S(1)}, u32[]{:S(2)}) copy-start(f32[1,512]{1,0:T(1,128)S(1)} %get-tuple-element.96) | copy-start | bytes 6148
  24.8 87.1 %copy-start.24 = (bf16[1,4,128,128]{2,3,1,0:T(8,128)(2,1)}, bf16[1,4,128,128]{2,3,1,0:T(8,128)(2,1)S(1)}, u32[]{:S(2)}) copy-start(bf16[1,4,128,128]{2,3,1,0:T(8,128)(2,1)S(1)} %copy.93) | copy-start | bytes 393220
  25.0 89.2 %copy-start.26 = (bf16[1,4,128,128]{2,3,1,0:T(8,128)(2,1)}, bf16[1,4,128,128]{2,3,1,0:T(8,128)(2,1)S(1)}, u32[]{:S(2)}) copy-start(bf16[1,4,128,128]{2,3,1,0:T(8,128)(2,1)S(1)} %copy.94) | copy-start | bytes 393220
  25.0 93.9 %copy-start.37 = (f32[1,512]{1,0:T(1,128)}, f32[1,512]{1,0:T(1,128)S(1)}, u32[]{:S(2)}) copy-start(f32[1,512]{1,0:T(1,128)S(1)} %get-tuple-element.101) | copy-start | bytes 6148
  25.0 93.9 %copy-start.42 = (f32[1,512]{1,0:T(1,128)}, f32[1,512]{1,0:T(1,128)S(1)}, u32[]{:S(2)}) copy-start(f32[1,512]{1,0:T(1,128)S(1)} %get-tuple-element.102) | copy-start | bytes 6148
  25.6 93.3 %copy-start.44 = (f32[512]{0:T(512)}, f32[512]{0:T(512)S(1)}, u32[]{:S(2)}) copy-start(f32[512]{0:T(512)S(1)} %get-tuple-element.107) | copy-start | bytes 6148
  25.6 84.3 %copy-start.90 = (f32[512]{0:T(512)S(1)}, f32[512]{0:T(512)}, u32[]{:S(2)}) copy-start(f32[512]{0:T(512)} %param.20) | copy-start | bytes 6148
  335.9 113.5 %copy-start.31 = (f32[1536]{0:T(1024)S(1)}, f32[1536]{0:T(1024)}, u32[]{:S(2)}) copy-start(f32[1536]{0:T(1024)} %param.25) | copy-start | bytes 18436
  335.9 185.6 %all-gather.20.cloned.1.call-start = ((), (), s32[]{:S(2)}) async-start(), calls=%async_computation.17 | async-start | bytes 3981312 | tf_op jit(solution)/shard_map/all_gather | solution.py:136
  336.5 222.0 %all-gather.18.cloned.1.call-start = ((), (), s32[]{:S(2)}) async-start(), calls=%async_computation.16 | async-start | bytes 3932160 | tf_op jit(solution)/shard_map/all_gather | solution.py:142
  448.3 434.6 %copy-start.51 = (f32[256]{0:T(256)}, f32[256]{0:T(256)S(1)}, u32[]{:S(2)}) copy-start(f32[256]{0:T(256)S(1)} %add_rsqrt_fusion) | copy-start | bytes 3076
  450.5 143.2 %all-gather.22.cloned.1.call-start = ((), (), s32[]{:S(2)}) async-start(), calls=%async_computation.18 | async-start | bytes 3981312 | tf_op jit(solution)/shard_map/all_gather | solution.py:137
  451.3 178.4 %all-gather.24.cloned.1.call-start = ((), (), s32[]{:S(2)}) async-start(), calls=%async_computation.19 | async-start | bytes 3981312 | tf_op jit(solution)/shard_map/all_gather | solution.py:138
  452.0 312.1 %reduce-scatter.16.cloned.1.call-start = ((), (), s32[]{:S(2)}) async-start(), calls=%async_computation.21 | async-start | bytes 7864320 | tf_op jit(solution)/shard_map/reduce_scatter | solution.py:171
  452.1 22.6 %collective-permute-start = (bf16[256,1536]{1,0:T(8,128)(2,1)}, bf16[256,1536]{1,0:T(8,128)(2,1)}, u32[]{:S(2)}, u32[]{:S(2)}) collective-permute-start(bf16[256,1536]{1,0:T(8,128)(2,1)} %param.29), channel_id=1, source_target_pairs={{0,1},{1,2},{2,3},{3,0},{4,5},{5,6},{6,7},{7,4},{8,9},{9,10},{10,1... | collective-permute-start | bytes 2359304 | tf_op jit(solution)/shard_map/ppermute | solution.py:20
  453.6 40.5 %collective-permute-start.1 = (bf16[256,1536]{1,0:T(8,128)(2,1)}, bf16[256,1536]{1,0:T(8,128)(2,1)}, u32[]{:S(2)}, u32[]{:S(2)}) collective-permute-start(bf16[256,1536]{1,0:T(8,128)(2,1)} %param.29), channel_id=1, source_target_pairs={{0,3},{1,0},{2,1},{3,2},{4,7},{5,4},{6,5},{7,6},{8,11},{9,8},{10,9... | collective-permute-start | bytes 2359304 | tf_op jit(solution)/shard_map/ppermute | solution.py:25
  474.7 44.8 %collective-permute-start.2 = (bf16[256,1536]{1,0:T(8,128)(2,1)}, bf16[256,1536]{1,0:T(8,128)(2,1)}, u32[]{:S(2)}, u32[]{:S(2)}) collective-permute-start(bf16[256,1536]{1,0:T(8,128)(2,1)} %collective-permute-done), channel_id=1, source_target_pairs={{0,1},{1,2},{2,3},{3,0},{4,5},{5,6},{6,7},{7,4},{8,9},{9,10},{10,1... | collective-permute-start | bytes 2359304 | tf_op jit(solution)/shard_map/ppermute | solution.py:20
  653.2 224.5 %reduce-scatter.14.cloned.1.call-start = ((), (), s32[]{:S(2)}) async-start(), calls=%async_computation.20 | async-start | bytes 7864320 | tf_op jit(solution)/shard_map/reduce_scatter | solution.py:146
  662.9 285.6 %all-gather.26.cloned.1.call-start = ((), (), s32[]{:S(2)}) async-start(), calls=%async_computation.22 | async-start | bytes 3932160 | tf_op jit(solution)/shard_map/all_gather | solution.py:180
  884.4 454.8 %all-reduce.47.cloned.1.call-start = ((), (), s32[]{:S(2)}) async-start(), calls=%async_computation.26 | async-start | bytes 131072 | tf_op jit(solution)/shard_map/psum | solution.py:249
  1083.5 16.5 copy-start.83
  1083.5 16.6 copy-start.40
  1083.6 16.6 copy-start.41
  1083.6 16.6 copy-start.81
  1222.9 230.1 %reduce-scatter.18.cloned.1.call-start = ((), (), s32[]{:S(2)}) async-start(), calls=%async_computation.23 | async-start | bytes 7864320 | tf_op jit(solution)/shard_map/reduce_scatter | solution.py:231
  1236.1 287.5 %reduce-scatter.28.cloned.1.call-start = ((), (), s32[]{:S(2)}) async-start(), calls=%async_computation.29 | async-start | bytes 7962624 | tf_op jit(solution)/shard_map/reduce_scatter | solution.py:260
  1245.9 347.5 %reduce-scatter.30.cloned.1.call-start = ((), (), s32[]{:S(2)}) async-start(), calls=%async_computation.30 | async-start | bytes 7962624 | tf_op jit(solution)/shard_map/reduce_scatter | solution.py:261
  1255.8 407.0 %reduce-scatter.32.cloned.1.call-start = ((), (), s32[]{:S(2)}) async-start(), calls=%async_computation.31 | async-start | bytes 7962624 | tf_op jit(solution)/shard_map/reduce_scatter | solution.py:262
  1265.9 434.9 %reduce-scatter.24.cloned.1.call-start = ((), (), s32[]{:S(2)}) async-start(), calls=%async_computation.27 | async-start | bytes 589824 | tf_op jit(solution)/shard_map/reduce_scatter | solution.py:259
  1268.9 482.1 %reduce-scatter.20.cloned.1.call-start = ((), (), s32[]{:S(2)}) async-start(), calls=%async_computation.24 | async-start | bytes 3538944 | tf_op jit(solution)/shard_map/reduce_scatter | solution.py:256
  1274.3 527.1 %reduce-scatter.26.cloned.1.call-start = ((), (), s32[]{:S(2)}) async-start(), calls=%async_computation.28 | async-start | bytes 3538944 | tf_op jit(solution)/shard_map/reduce_scatter | solution.py:258
  1281.0 570.7 %reduce-scatter.22.cloned.1.call-start = ((), (), s32[]{:S(2)}) async-start(), calls=%async_computation.25 | async-start | bytes 3538944 | tf_op jit(solution)/shard_map/reduce_scatter | solution.py:257
  1287.6 165.4 %copy-start.6 = (bf16[256,1536]{1,0:T(8,128)(2,1)S(1)}, bf16[256,1536]{1,0:T(8,128)(2,1)}, u32[]{:S(2)}) copy-start(bf16[256,1536]{1,0:T(8,128)(2,1)} %param.15) | copy-start | bytes 2359300
  1287.6 165.4 %copy-start.36 = (f32[1536]{0:T(1024)S(1)}, f32[1536]{0:T(1024)}, u32[]{:S(2)}) copy-start(f32[1536]{0:T(1024)} %param.16) | copy-start | bytes 18436
  1287.6 165.4 %copy-start.66 = (f32[256]{0:T(256)S(1)}, f32[256]{0:T(256)}, u32[]{:S(2)}) copy-start(f32[256]{0:T(256)} %copy-done.65) | copy-start | bytes 3076
  1287.6 209.6 %copy-start.3 = (f32[256,1536]{1,0:T(8,128)S(1)}, f32[256,1536]{1,0:T(8,128)}, u32[]{:S(2)}) copy-start(f32[256,1536]{1,0:T(8,128)} %copy-done.1) | copy-start | bytes 4718596
  1287.6 209.6 %copy-start.20 = (bf16[256,1536]{1,0:T(8,128)(2,1)S(1)}, bf16[256,1536]{1,0:T(8,128)(2,1)}, u32[]{:S(2)}) copy-start(bf16[256,1536]{1,0:T(8,128)(2,1)} %param.29) | copy-start | bytes 2359300
  1287.6 209.6 %copy-start.52 = (f32[256]{0:T(256)S(1)}, f32[256]{0:T(256)}, u32[]{:S(2)}) copy-start(f32[256]{0:T(256)} %copy-done.51) | copy-start | bytes 3076
  1287.6 209.6 %copy-start.68 = (f32[256]{0:T(256)S(1)}, f32[256]{0:T(256)}, u32[]{:S(2)}) copy-start(f32[256]{0:T(256)} %copy-done.67) | copy-start | bytes 3076
  (72 other events, 522.5 us)
Sparse Core Ops, SparseCore 0:
  9.9 28.7 all-gather.11
  40.8 63.4 all-gather.9
  106.3 24.3 all-gather.13
  132.4 25.6 all-gather.15
  336.1 109.4 reduce-scatter.11
  447.3 34.4 all-gather.19
  483.9 74.5 all-gather.17
  560.4 33.2 all-gather.21
  595.6 33.9 all-gather.23
  653.3 110.7 reduce-scatter.15
  766.4 111.2 reduce-scatter.13
  884.5 64.0 all-gather.25
  1223.0 116.1 all-reduce.46
  1341.4 111.5 reduce-scatter.17
  1456.9 66.5 reduce-scatter.27
  1527.9 65.4 reduce-scatter.29
  1597.4 65.4 reduce-scatter.31
  1666.7 34.0 reduce-scatter.23
  1704.8 46.2 reduce-scatter.19
  1755.2 46.2 reduce-scatter.25
  1805.4 46.2 reduce-scatter.21
